TPU v7x, 32 devices: a whole 2x2x4 slice. The times are simulated.
32 devices in a mesh: img: 8 (over y, x, core), feat: 4 (over z).
Axes of the slice: x: 2, y: 2, z: 4, core: 2. Of those that a mesh axis runs over, the one named last changes fastest.
Arguments:
- coeffs: bfloat16 [16384, 512], P('img', 'feat'), may hold values from -16 to 16
- triples: int32 [3, 16384], P(None, 'feat'), may hold values from 0 to 510, as said below
- sketch: int32 [16384, 128], P('feat'), may hold values from -1 to 1
Outputs:
- basis: float32 [16384, 128], P('img')
- projected: float32 [128, 16384], P('img', 'feat')
Inputs may be any that keep to these rules, and one draw needn't show every extreme that they name: `triples`: every column is a triple k1, k2, k1 + k2 with k1 and k2 below 256.
All inputs are finite; a program needn't handle non-finite values.
Results may differ from a plain program's by a relative error of at most 0.0044.
Values may be sent and summed in bfloat16 or wider, within the bound.
A program may use at most 192 MiB of HBM per device.

v0:
```python
import functools

import jax
import jax.numpy as jnp
from jax import lax
from jax.experimental import pallas as pl
from jax.experimental.pallas import tpu as pltpu
from jax.sharding import PartitionSpec as P

CHUNKS = 8
MESH = pl.DeviceIdType.MESH
VMEM = pl.BlockSpec(memory_space=pltpu.VMEM)


def greet(axis, peers):
    barrier = pltpu.get_barrier_semaphore()
    for peer in peers:
        pl.semaphore_signal(barrier, inc=1, device_id={axis: peer}, device_id_type=MESH)
    pl.semaphore_wait(barrier, len(peers))


def gather_kernel(count, width, coeffs_ref, sel_ref, signs_ref, tile_ref, sum_ref, blocks, own_sem, send_sem, recv_sem):
    me = lax.axis_index("feat")
    rows, part = coeffs_ref.shape
    step = rows // CHUNKS
    half = count * part // 2
    tiles = signs_ref.shape[0] // width
    barrier = pltpu.get_barrier_semaphore()

    @pl.when(me > 0)
    def _():
        pl.semaphore_signal(barrier, inc=1, device_id={"feat": me - 1}, device_id_type=MESH)

    @pl.when(me < count - 1)
    def _():
        pl.semaphore_signal(barrier, inc=1, device_id={"feat": me + 1}, device_id_type=MESH)

    own = pltpu.make_async_copy(coeffs_ref, blocks.at[me], own_sem)
    own.start()

    @pl.when((me > 0) & (me < count - 1))
    def _():
        pl.semaphore_wait(barrier, 2)

    @pl.when((me == 0) | (me == count - 1))
    def _():
        pl.semaphore_wait(barrier, 1)

    own.wait()

    def copy(side, hop, chunk, source, target):
        span = blocks.at[source, pl.ds(pl.multiple_of(chunk * step, step), step)]
        return pltpu.make_async_remote_copy(
            src_ref=span,
            dst_ref=span,
            send_sem=send_sem.at[side, hop, chunk],
            recv_sem=recv_sem.at[side, hop, chunk],
            device_id={"feat": target},
            device_id_type=MESH,
        )

    def one_round(turn, carry):
        for hop in range(count):
            chunk = turn - hop
            live = (chunk >= 0) & (chunk < CHUNKS)
            if hop > 0:

                @pl.when(live & (me >= hop))
                def _():
                    copy(0, hop - 1, chunk, me - hop, me - 1).wait_recv()

                @pl.when(live & (me + hop < count))
                def _():
                    copy(1, hop - 1, chunk, me + hop, me + 1).wait_recv()

            if hop < count - 1:

                @pl.when(live & (me >= hop) & (me < count - 1))
                def _():
                    copy(0, hop, chunk, me - hop, me + 1).start()

                @pl.when(live & (me + hop < count) & (me > 0))
                def _():
                    copy(1, hop, chunk, me + hop, me - 1).start()

        @pl.when(turn >= count - 1)
        def _():
            first_row = pl.multiple_of((turn - (count - 1)) * step, step)
            here = pl.ds(first_row, step)
            sum_ref[here, :] = jnp.zeros((step, sum_ref.shape[1]), jnp.float32)
            low = jnp.concatenate([blocks[s, here, :] for s in range(count // 2)], axis=1)
            high = jnp.concatenate([blocks[s, here, :] for s in range(count // 2, count)], axis=1)
            full = jnp.concatenate([low, high], axis=1)

            def one_tile(j, unused):
                cols = pl.ds(pl.multiple_of(j * width, width), width)
                first = jnp.dot(low, sel_ref[:half, cols], preferred_element_type=jnp.float32)
                second = jnp.dot(low, sel_ref[half : 2 * half, cols], preferred_element_type=jnp.float32)
                third = jnp.dot(full, sel_ref[2 * half :, cols], preferred_element_type=jnp.float32)
                tile = (first * second * third).astype(jnp.bfloat16)
                tile_ref[here, cols] = tile
                sum_ref[here, :] += jnp.dot(tile, signs_ref[cols, :], preferred_element_type=jnp.float32)
                return unused

            lax.fori_loop(0, tiles, one_tile, 0)

        return carry

    lax.fori_loop(0, CHUNKS + count - 1, one_round, 0)

    def drain(chunk, carry):
        for hop in range(count - 1):

            @pl.when((me >= hop) & (me < count - 1))
            def _():
                copy(0, hop, chunk, me - hop, me + 1).wait_send()

            @pl.when((me + hop < count) & (me > 0))
            def _():
                copy(1, hop, chunk, me + hop, me - 1).wait_send()

        return carry

    lax.fori_loop(0, CHUNKS, drain, 0)


def gather_features(coeffs, selectors, signs, count):
    rows, part = coeffs.shape
    feats, rank = signs.shape
    hops = max(count - 1, 1)
    return pl.pallas_call(
        functools.partial(gather_kernel, count, min(512, feats)),
        in_specs=[VMEM] * 3,
        out_specs=[VMEM] * 2,
        out_shape=[
            jax.ShapeDtypeStruct((rows, feats), jnp.bfloat16),
            jax.ShapeDtypeStruct((rows, rank), jnp.float32),
        ],
        scratch_shapes=[
            pltpu.VMEM((count, rows, part), jnp.bfloat16),
            pltpu.SemaphoreType.DMA,
            pltpu.SemaphoreType.DMA((2, hops, CHUNKS)),
            pltpu.SemaphoreType.DMA((2, hops, CHUNKS)),
        ],
        compiler_params=pltpu.CompilerParams(
            collective_id=0, has_side_effects=True, vmem_limit_bytes=48 << 20
        ),
    )(coeffs, selectors, signs)


def peers_of(me, count):
    return [lax.rem(me + k, count) for k in range(1, count)]


def sum_gather_kernel(count, part_ref, out_ref, slots, full, send_sem, recv_sem, send_again, recv_again):
    me = lax.axis_index("feat")
    peers = peers_of(me, count)
    greet("feat", peers)
    copies = []
    for k, peer in enumerate(peers):
        copies.append(
            pltpu.make_async_remote_copy(
                src_ref=part_ref.at[peer],
                dst_ref=slots.at[k],
                send_sem=send_sem.at[k],
                recv_sem=recv_sem.at[k],
                device_id={"feat": peer},
                device_id_type=MESH,
            )
        )
        copies[-1].start()
    total = part_ref[me].astype(jnp.float32)
    for k, copy in enumerate(copies):
        copy.wait_recv()
        total = total + slots[k].astype(jnp.float32)
    full[me] = total.astype(full.dtype)
    again = []
    for k, peer in enumerate(peers):
        again.append(
            pltpu.make_async_remote_copy(
                src_ref=full.at[me],
                dst_ref=full.at[me],
                send_sem=send_again.at[k],
                recv_sem=recv_again.at[k],
                device_id={"feat": peer},
                device_id_type=MESH,
            )
        )
        again[-1].start()
    for k in range(count - 1):
        source = lax.rem(me + count - 1 - k, count)
        pltpu.make_async_remote_copy(
            src_ref=full.at[source],
            dst_ref=full.at[source],
            send_sem=send_again.at[k],
            recv_sem=recv_again.at[k],
            device_id={"feat": peers[k]},
            device_id_type=MESH,
        ).wait_recv()
    out_ref[...] = full[...]
    for copy in copies + again:
        copy.wait_send()


def sum_gather(part, count):
    rows, rank = part.shape
    blocks = part.reshape(count, rows // count, rank)
    others = max(count - 1, 1)
    out = pl.pallas_call(
        functools.partial(sum_gather_kernel, count),
        in_specs=[VMEM],
        out_specs=VMEM,
        out_shape=jax.ShapeDtypeStruct(blocks.shape, part.dtype),
        scratch_shapes=[
            pltpu.VMEM((others,) + blocks.shape[1:], part.dtype),
            pltpu.VMEM(blocks.shape, part.dtype),
        ]
        + [pltpu.SemaphoreType.DMA((others,))] * 4,
        compiler_params=pltpu.CompilerParams(collective_id=1, has_side_effects=True),
    )(blocks)
    return out.reshape(rows, rank)


def exchange_kernel(count, scatter, part_ref, out_ref, slots, send_sem, recv_sem):
    me = lax.axis_index("img")
    peers = peers_of(me, count)
    greet("img", peers)
    copies = []
    for k, peer in enumerate(peers):
        copies.append(
            pltpu.make_async_remote_copy(
                src_ref=part_ref.at[peer] if scatter else part_ref,
                dst_ref=slots.at[k],
                send_sem=send_sem.at[k],
                recv_sem=recv_sem.at[k],
                device_id={"img": peer},
                device_id_type=MESH,
            )
        )
        copies[-1].start()
    if scatter:
        out_ref[...] = part_ref[me].astype(jnp.float32)
    else:
        slots[count - 1] = part_ref[...]
    for copy in copies:
        copy.wait_recv()
    if scatter:
        for k in range(count - 1):
            out_ref[...] += slots[k].astype(jnp.float32)
    else:
        total = jnp.zeros(out_ref.shape, jnp.float32)
        for sender in range(count):
            slot = lax.rem(me + 2 * count - sender - 1, count)
            total = total + slots[slot]
        out_ref[...] = total
    for copy in copies:
        copy.wait_send()


def exchange(part, count, scatter, collective_id):
    shape = part.shape[1:] if scatter else part.shape
    others = max(count - 1, 1)
    return pl.pallas_call(
        functools.partial(exchange_kernel, count, scatter),
        in_specs=[VMEM],
        out_specs=VMEM,
        out_shape=jax.ShapeDtypeStruct(shape, jnp.float32),
        scratch_shapes=[
            pltpu.VMEM((others + (0 if scatter else 1),) + shape, part.dtype),
            pltpu.SemaphoreType.DMA((others,)),
            pltpu.SemaphoreType.DMA((others,)),
        ],
        compiler_params=pltpu.CompilerParams(collective_id=collective_id, has_side_effects=True),
    )(part)


def on_device(coeffs, triples, sketch):
    rows_here = coeffs.shape[0]
    feats_here = triples.shape[1]
    rank_cols = sketch.shape[1]
    img_count = lax.axis_size("img")
    feat_count = lax.axis_size("feat")
    total_rows = rows_here * img_count
    total_feats = feats_here * feat_count
    coef_total = coeffs.shape[1] * feat_count
    half = coef_total // 2

    def selector(index, depth):
        levels = lax.broadcasted_iota(jnp.int32, (depth, feats_here), 0)
        return (levels == triples[index][None, :]).astype(jnp.bfloat16)

    selectors = jnp.concatenate([selector(0, half), selector(1, half), selector(2, coef_total)], axis=0)
    signs = sketch.astype(jnp.bfloat16)
    tiles, part = gather_features(coeffs, selectors, signs, feat_count)
    value = sum_gather(part.astype(jnp.bfloat16), feat_count)
    contract = (((0,), (0,)), ((), ()))
    gram = lax.dot_general(value, value, contract, preferred_element_type=jnp.float32)
    sketch_scale = (1.5 / total_feats) ** 0.5
    gram = exchange(gram, img_count, False, 2) * (sketch_scale * sketch_scale / total_rows)
    raw = lax.dot_general(value, tiles, contract, preferred_element_type=jnp.float32)
    lower = jnp.linalg.cholesky(gram)
    inverse = lax.linalg.triangular_solve(
        lower, jnp.eye(rank_cols, dtype=jnp.float32), left_side=True, lower=True
    ) * sketch_scale
    exact = lax.Precision.HIGHEST
    solved = jnp.dot(inverse, raw, precision=exact) / jnp.sqrt(jnp.float32(total_rows))
    outgoing = solved.astype(jnp.bfloat16).reshape(img_count, rank_cols // img_count, feats_here)
    projected = exchange(outgoing, img_count, True, 3)
    basis = jnp.dot(value.astype(jnp.float32), inverse.T, precision=exact)
    return (basis, projected)


def solution(mesh):
    in_specs = (P("img", "feat"), P(None, "feat"), P("feat", None))
    out_specs = (P("img", None), P("img", "feat"))
    return jax.shard_map(
        on_device, mesh=mesh, in_specs=in_specs, out_specs=out_specs, check_vma=False
    )
```

profile of v0, /device:TPU:1, one launch (start us, length us, event | category | flops | bytes accessed | tf_op | source)
XLA Modules:
  0.0 166.0 jit_solution(14986299393577600722)
XLA Ops:
  0.6 1.0 fusion.4
  1.6 1.7 %convert_element_type.6.signs_ref = bf16[4096,128]{1,0:T(8,128)(2,1)S(1)} convert(s32[4096,128]{1,0:T(8,128)} %param.5) | non-fusion elementwise | flops 524288 | bytes 3145728 | tf_op jit(solution)/shard_map/convert_element_type | solution.py:293
  3.3 1.1 iota_compare_fusion.1
  4.4 1.3 iota_compare_fusion
  5.7 0.0 copy-start
  5.7 4.7 %add_convert_fusion.sel_ref = bf16[1024,4096]{1,0:T(8,128)(2,1)} fusion(pred[512,4096]{1,0:T(8,128)(4,1)S(1)} %iota_compare_fusion, pred[256,4096]{1,0:T(8,128)(4,1)S(1)} %get-tuple-element.9, pred[256,4096]{1,0:T(8,128)(4,1)S(1)} %get-tuple-element.10), kind=kLoop, calls=%fused_computation | loop fusion | flops 12582912 | bytes 12582912 | tf_op jit(solution)/shard_map/concatenate | solution.py:292
  10.4 0.0 copy-done
  10.4 60.7 %shard_map.50 = (bf16[2048,4096]{1,0:T(8,128)(2,1)}, f32[2048,128]{1,0:T(8,128)S(1)}) custom-call(bf16[2048,128]{1,0:T(8,128)(2,1)S(1)} %copy-done, bf16[1024,4096]{1,0:T(8,128)(2,1)} %add_convert_fusion.sel_ref, bf16[4096,128]{1,0:T(8,128)(2,1)S(1)} %convert_element_type.6.signs_ref), custom_call_target="tpu_custom_call" | custom-call | tf_op jit(solution)/shard_map/pallas_call | solution.py:131
  71.1 0.8 convert_element_type.7
  71.9 20.7 %shard_map.51 = bf16[4,512,128]{2,1,0:T(8,128)(2,1)} custom-call(bf16[4,512,128]{2,1,0:T(8,128)(2,1)} %bitcast.28), custom_call_target="tpu_custom_call" | custom-call | tf_op jit(solution)/shard_map/pallas_call | solution.py:209
  92.6 0.0 copy-start.1
  92.6 8.4 %fusion.6 = f32[128,4096]{1,0:T(8,128)S(1)} fusion(bf16[2048,128]{1,0:T(8,128)(2,1)} %bitcast.25, bf16[2048,4096]{1,0:T(8,128)(2,1)} %get-tuple-element.5), kind=kOutput, calls=%fused_computation.20 | convolution fusion | flops 2147483648 | bytes 19398656 | tf_op jit(solution)/shard_map/dot_general | solution.py:300
  100.9 0.0 copy-done.1
  101.0 1.0 convolution_bitcast_fusion.part_ref
  101.9 17.0 %shard_map.52 = f32[128,128]{1,0:T(8,128)} custom-call(f32[128,128]{1,0:T(8,128)} %convolution_bitcast_fusion.part_ref), custom_call_target="tpu_custom_call" | custom-call | tf_op jit(solution)/shard_map/pallas_call | solution.py:263
  118.9 0.9 copy.6
  119.9 0.1 copy.7
  120.0 11.7 %cholesky.17 = f32[128,128]{1,0:T(8,128)S(1)} custom-call(f32[128,128]{1,0:T(8,128)S(1)} %fusion.3), custom_call_target="Cholesky" | custom-call | tf_op jit(solution)/shard_map/jit(cholesky)/cholesky | solution.py:301
  131.7 0.6 compare_reduce_fusion
  132.4 0.7 fusion.1
  133.0 9.8 %custom-call.6 = f32[1,128,128]{1,2,0:T(8,128)S(1)} custom-call(f32[1,128,128]{2,1,0:T(8,128)S(1)} %fusion.1), custom_call_target="InvertDiagBlocksLowerTriangular" | custom-call | tf_op jit(solution)/shard_map/triangular_solve | solution.py:302
  142.8 0.3 convolution_multiply_fusion.1
  143.1 2.9 %fusion = bf16[128,4096]{1,0:T(8,128)(2,1)} fusion(f32[128,128]{1,0:T(8,128)S(1)} %convolution_multiply_fusion.1, f32[128,4096]{1,0:T(8,128)S(1)} %fusion.6), kind=kOutput, calls=%fused_computation.3 | convolution fusion | flops 806354944 | bytes 3211264 | tf_op jit(solution)/shard_map/dot_general | solution.py:306
  146.0 16.8 %shard_map.53 = f32[16,4096]{1,0:T(8,128)} custom-call(bf16[8,16,4096]{2,1,0:T(8,128)(2,1)} %bitcast.27), custom_call_target="tpu_custom_call" | custom-call | tf_op jit(solution)/shard_map/pallas_call | solution.py:263
  162.8 1.6 fusion.5
  164.3 1.7 %copy.10 = f32[16,4096]{1,0:T(8,128)} copy(f32[16,4096]{1,0:T(8,128)} %shard_map.53) | data formatting | bytes 524288
  (3 shorter events, 0.1 us)
Async XLA Ops:
  5.7 4.7 %copy-start = (bf16[2048,128]{1,0:T(8,128)(2,1)S(1)}, bf16[2048,128]{1,0:T(8,128)(2,1)}, u32[]{:S(2)}) copy-start(bf16[2048,128]{1,0:T(8,128)(2,1)} %coeffs_ref.1) | copy-start | bytes 1572868
  92.6 8.4 %copy-start.1 = (bf16[4,512,128]{2,1,0:T(8,128)(2,1)S(1)}, bf16[4,512,128]{2,1,0:T(8,128)(2,1)}, u32[]{:S(2)}) copy-start(bf16[4,512,128]{2,1,0:T(8,128)(2,1)} %shard_map.51) | copy-start | bytes 1572868
where the time goes:
time: 166 us
  Pallas kernels  115 us (69%)
  other arithmetic  32.4 us (20%)
  matrix products  14 us (8%)
  local copies, waits for them, and re-layouts  3.7 us (2%)
    pallas_call x1, Pallas kernels, gather_features(): pl.pallas_call(functools.partial(gather_kernel, count, min(512, feats)),...  60.7 us
    pallas_call x2, Pallas kernels, exchange(): pl.pallas_call(functools.partial(exchange_kernel, count, scatter), in_spe...  33.8 us
    pallas_call x1, Pallas kernels, sum_gather(): pl.pallas_call(functools.partial(sum_gather_kernel, count), in_specs=[VME...  20.7 us
    another operation x3, other arithmetic, on_device(): lower = jnp.linalg.cholesky(gram)  12.4 us
    another operation x2, other arithmetic, on_device(): lax.linalg.triangular_solve(lower, jnp.eye(rank_cols, dtype=jnp.float32),...  10.5 us
    dot_general x1, matrix products, on_device(): lax.dot_general(value, tiles, contract, preferred_element_type=jnp.float32)  8.35 us
    concatenate x1, other arithmetic, on_device(): jnp.concatenate([selector(0, half), selector(1, half), selector(2, coef_t...  4.66 us

commit v1 on v0

--- a/solution.py
+++ b/solution.py
@@ -19,12 +19,30 @@
     pl.semaphore_wait(barrier, len(peers))
 
 
-def gather_kernel(count, width, coeffs_ref, sel_ref, signs_ref, tile_ref, sum_ref, blocks, own_sem, send_sem, recv_sem):
+def gather_kernel(
+    count, width, coeffs_ref, triples_ref, sketch_ref, tile_ref, sum_ref, blocks, sel_ref, signs_ref, own_sem, send_sem, recv_sem
+):
     me = lax.axis_index("feat")
     rows, part = coeffs_ref.shape
     step = rows // CHUNKS
     half = count * part // 2
-    tiles = signs_ref.shape[0] // width
+    tiles = sketch_ref.shape[0] // width
+    spans = ((0, half), (half, half), (2 * half, 2 * half))
+
+    def build(index):
+        start, depth = spans[index]
+
+        def one(j, carry):
+            cols = pl.ds(pl.multiple_of(j * width, width), width)
+            levels = lax.broadcasted_iota(jnp.int32, (depth, width), 0)
+            chosen = triples_ref[index : index + 1, cols]
+            sel_ref[start : start + depth, cols] = jnp.where(levels == chosen, 1.0, 0.0).astype(jnp.bfloat16)
+            if index == 0:
+                signs_ref[cols, :] = sketch_ref[cols, :].astype(jnp.float32).astype(jnp.bfloat16)
+            return carry
+
+        lax.fori_loop(0, tiles, one, 0)
+
     barrier = pltpu.get_barrier_semaphore()
 
     @pl.when(me > 0)
@@ -83,6 +101,12 @@
                 def _():
                     copy(1, hop, chunk, me + hop, me - 1).start()
 
+        for index in range(3):
+
+            @pl.when(turn == min(index, count - 2))
+            def _():
+                build(index)
+
         @pl.when(turn >= count - 1)
         def _():
             first_row = pl.multiple_of((turn - (count - 1)) * step, step)
@@ -102,7 +126,7 @@
                 sum_ref[here, :] += jnp.dot(tile, signs_ref[cols, :], preferred_element_type=jnp.float32)
                 return unused
 
-            lax.fori_loop(0, tiles, one_tile, 0)
+            lax.fori_loop(0, tiles, one_tile, 0, unroll=2)
 
         return carry
 
@@ -124,9 +148,9 @@
     lax.fori_loop(0, CHUNKS, drain, 0)
 
 
-def gather_features(coeffs, selectors, signs, count):
+def gather_features(coeffs, triples, sketch, count):
     rows, part = coeffs.shape
-    feats, rank = signs.shape
+    feats, rank = sketch.shape
     hops = max(count - 1, 1)
     return pl.pallas_call(
         functools.partial(gather_kernel, count, min(512, feats)),
@@ -138,14 +162,16 @@
         ],
         scratch_shapes=[
             pltpu.VMEM((count, rows, part), jnp.bfloat16),
+            pltpu.VMEM((2 * count * part, feats), jnp.bfloat16),
+            pltpu.VMEM((feats, rank), jnp.bfloat16),
             pltpu.SemaphoreType.DMA,
             pltpu.SemaphoreType.DMA((2, hops, CHUNKS)),
             pltpu.SemaphoreType.DMA((2, hops, CHUNKS)),
         ],
         compiler_params=pltpu.CompilerParams(
-            collective_id=0, has_side_effects=True, vmem_limit_bytes=48 << 20
+            collective_id=0, has_side_effects=True, vmem_limit_bytes=24 << 20
         ),
-    )(coeffs, selectors, signs)
+    )(coeffs, triples, sketch)
 
 
 def peers_of(me, count):
@@ -216,12 +242,72 @@
             pltpu.VMEM(blocks.shape, part.dtype),
         ]
         + [pltpu.SemaphoreType.DMA((others,))] * 4,
-        compiler_params=pltpu.CompilerParams(collective_id=1, has_side_effects=True),
+        compiler_params=pltpu.CompilerParams(collective_id=1, has_side_effects=True, vmem_limit_bytes=8 << 20),
     )(blocks)
     return out.reshape(rows, rank)
 
 
-def exchange_kernel(count, scatter, part_ref, out_ref, slots, send_sem, recv_sem):
+def gram_kernel(count, width, value_ref, tile_ref, gram_ref, raw_ref, turned, slots, send_sem, recv_sem):
+    me = lax.axis_index("img")
+    peers = peers_of(me, count)
+    turned[...] = value_ref[...].T
+    slots[count - 1] = jnp.dot(turned[...], value_ref[...], preferred_element_type=jnp.float32)
+    greet("img", peers)
+    copies = []
+    for k, peer in enumerate(peers):
+        copies.append(
+            pltpu.make_async_remote_copy(
+                src_ref=slots.at[count - 1],
+                dst_ref=slots.at[k],
+                send_sem=send_sem.at[k],
+                recv_sem=recv_sem.at[k],
+                device_id={"img": peer},
+                device_id_type=MESH,
+            )
+        )
+        copies[-1].start()
+
+    def one_tile(j, carry):
+        cols = pl.ds(pl.multiple_of(j * width, width), width)
+        raw_ref[:, cols] = jnp.dot(turned[...], tile_ref[:, cols], preferred_element_type=jnp.float32)
+        return carry
+
+    lax.fori_loop(0, tile_ref.shape[1] // width, one_tile, 0)
+    for copy in copies:
+        copy.wait_recv()
+    total = jnp.zeros(gram_ref.shape, jnp.float32)
+    for sender in range(count):
+        total = total + slots[lax.rem(me + 2 * count - sender - 1, count)]
+    gram_ref[...] = total
+    for copy in copies:
+        copy.wait_send()
+
+
+def gram_and_raw(value, tiles, count):
+    rows, rank = value.shape
+    feats = tiles.shape[1]
+    others = max(count - 1, 1)
+    return pl.pallas_call(
+        functools.partial(gram_kernel, count, min(512, feats)),
+        in_specs=[VMEM] * 2,
+        out_specs=[VMEM] * 2,
+        out_shape=[
+            jax.ShapeDtypeStruct((rank, rank), jnp.float32),
+            jax.ShapeDtypeStruct((rank, feats), jnp.float32),
+        ],
+        scratch_shapes=[
+            pltpu.VMEM((rank, rows), jnp.bfloat16),
+            pltpu.VMEM((others + 1, rank, rank), jnp.float32),
+            pltpu.SemaphoreType.DMA((others,)),
+            pltpu.SemaphoreType.DMA((others,)),
+        ],
+        compiler_params=pltpu.CompilerParams(
+            collective_id=2, has_side_effects=True, vmem_limit_bytes=16 << 20
+        ),
+    )(value, tiles)
+
+
+def rows_kernel(count, part_ref, out_ref, slots, send_sem, recv_sem):
     me = lax.axis_index("img")
     peers = peers_of(me, count)
     greet("img", peers)
@@ -229,7 +315,7 @@
     for k, peer in enumerate(peers):
         copies.append(
             pltpu.make_async_remote_copy(
-                src_ref=part_ref.at[peer] if scatter else part_ref,
+                src_ref=part_ref.at[peer],
                 dst_ref=slots.at[k],
                 send_sem=send_sem.at[k],
                 recv_sem=recv_sem.at[k],
@@ -238,39 +324,28 @@
             )
         )
         copies[-1].start()
-    if scatter:
-        out_ref[...] = part_ref[me].astype(jnp.float32)
-    else:
-        slots[count - 1] = part_ref[...]
-    for copy in copies:
+    out_ref[...] = part_ref[me].astype(jnp.float32)
+    for k, copy in enumerate(copies):
         copy.wait_recv()
-    if scatter:
-        for k in range(count - 1):
-            out_ref[...] += slots[k].astype(jnp.float32)
-    else:
-        total = jnp.zeros(out_ref.shape, jnp.float32)
-        for sender in range(count):
-            slot = lax.rem(me + 2 * count - sender - 1, count)
-            total = total + slots[slot]
-        out_ref[...] = total
+        out_ref[...] += slots[k].astype(jnp.float32)
     for copy in copies:
         copy.wait_send()
 
 
-def exchange(part, count, scatter, collective_id):
-    shape = part.shape[1:] if scatter else part.shape
+def sum_rows(part, count):
+    shape = part.shape[1:]
     others = max(count - 1, 1)
     return pl.pallas_call(
-        functools.partial(exchange_kernel, count, scatter),
+        functools.partial(rows_kernel, count),
         in_specs=[VMEM],
         out_specs=VMEM,
         out_shape=jax.ShapeDtypeStruct(shape, jnp.float32),
         scratch_shapes=[
-            pltpu.VMEM((others + (0 if scatter else 1),) + shape, part.dtype),
+            pltpu.VMEM((others,) + shape, part.dtype),
             pltpu.SemaphoreType.DMA((others,)),
             pltpu.SemaphoreType.DMA((others,)),
         ],
-        compiler_params=pltpu.CompilerParams(collective_id=collective_id, has_side_effects=True),
+        compiler_params=pltpu.CompilerParams(collective_id=3, has_side_effects=True, vmem_limit_bytes=12 << 20),
     )(part)
 
 
@@ -282,22 +357,11 @@
     feat_count = lax.axis_size("feat")
     total_rows = rows_here * img_count
     total_feats = feats_here * feat_count
-    coef_total = coeffs.shape[1] * feat_count
-    half = coef_total // 2
-
-    def selector(index, depth):
-        levels = lax.broadcasted_iota(jnp.int32, (depth, feats_here), 0)
-        return (levels == triples[index][None, :]).astype(jnp.bfloat16)
-
-    selectors = jnp.concatenate([selector(0, half), selector(1, half), selector(2, coef_total)], axis=0)
-    signs = sketch.astype(jnp.bfloat16)
-    tiles, part = gather_features(coeffs, selectors, signs, feat_count)
+    tiles, part = gather_features(coeffs, triples, sketch, feat_count)
     value = sum_gather(part.astype(jnp.bfloat16), feat_count)
-    contract = (((0,), (0,)), ((), ()))
-    gram = lax.dot_general(value, value, contract, preferred_element_type=jnp.float32)
     sketch_scale = (1.5 / total_feats) ** 0.5
-    gram = exchange(gram, img_count, False, 2) * (sketch_scale * sketch_scale / total_rows)
-    raw = lax.dot_general(value, tiles, contract, preferred_element_type=jnp.float32)
+    gram, raw = gram_and_raw(value, tiles, img_count)
+    gram = gram * (sketch_scale * sketch_scale / total_rows)
     lower = jnp.linalg.cholesky(gram)
     inverse = lax.linalg.triangular_solve(
         lower, jnp.eye(rank_cols, dtype=jnp.float32), left_side=True, lower=True
@@ -305,7 +369,7 @@
     exact = lax.Precision.HIGHEST
     solved = jnp.dot(inverse, raw, precision=exact) / jnp.sqrt(jnp.float32(total_rows))
     outgoing = solved.astype(jnp.bfloat16).reshape(img_count, rank_cols // img_count, feats_here)
-    projected = exchange(outgoing, img_count, True, 3)
+    projected = sum_rows(outgoing, img_count)
     basis = jnp.dot(value.astype(jnp.float32), inverse.T, precision=exact)
     return (basis, projected)
 

time: 166 us -> 128 us (0.77)
  Pallas kernels: 115 us -> 96.4 us
  matrix products: 14 us -> 3.73 us
  other arithmetic: 32.4 us -> 22.9 us
    pallas_call x1, Pallas kernels: 60.7 us -> 46.7 us  [gather_features(): pl.pallas_call(functools.partial(gather_kernel, count, min(512, feats)),...]
    dot_general x2 -> x0, matrix products: 9.33 us -> none  [the longest x1 8.35 us: on_device(): lax.dot_general(value, tiles, contract, preferred_element_type=jnp.float32)]
    concatenate x1 -> x0, other arithmetic: 4.66 us -> none  [on_device(): jnp.concatenate([selector(0, half), selector(1, half), selector(2, coef_t...]
    pallas_call x2, Pallas kernels: 33.8 us -> 31.2 us  [the longest x1 16.4 us: gram_and_raw(): pl.pallas_call(functools.partial(gram_kernel, count, min(512, feats)), in...]
    unnamed x5 -> x7, local copies, waits for them, and re-layouts: 1.68 us -> 4.17 us
    eq x2 -> x0, other arithmetic: 2.34 us -> none  [selector(): return (levels == triples[index][None, :]).astype(jnp.bfloat16)]
    pallas_call x1, Pallas kernels: 20.7 us -> 18.5 us  [sum_gather(): pl.pallas_call(functools.partial(sum_gather_kernel, count), in_specs=[VME...]
    convert_element_type x1 -> x0, other arithmetic: 1.7 us -> none  [on_device(): signs = sketch.astype(jnp.bfloat16)]
where the time goes in v1:
time: 128 us
  Pallas kernels  96.4 us (75%)
  other arithmetic  22.9 us (18%)
  local copies, waits for them, and re-layouts  4.34 us (3%)
  matrix products  3.73 us (3%)
    pallas_call x1, Pallas kernels, gather_features(): pl.pallas_call(functools.partial(gather_kernel, count, min(512, feats)),...  46.7 us
    pallas_call x1, Pallas kernels, sum_gather(): pl.pallas_call(functools.partial(sum_gather_kernel, count), in_specs=[VME...  18.5 us
    pallas_call x1, Pallas kernels, gram_and_raw(): pl.pallas_call(functools.partial(gram_kernel, count, min(512, feats)), in...  16.4 us
    pallas_call x1, Pallas kernels, sum_rows(): pl.pallas_call(functools.partial(rows_kernel, count), in_specs=[VMEM], ou...  14.8 us
    another operation x3, other arithmetic, on_device(): lower = jnp.linalg.cholesky(gram)  12.4 us
    another operation x2, other arithmetic, on_device(): lax.linalg.triangular_solve(lower, jnp.eye(rank_cols, dtype=jnp.float32),...  10.5 us
    unnamed x7, local copies, waits for them, and re-layouts  4.17 us

profile of v1, /device:TPU:1, one launch (start us, length us, event | category | flops | bytes accessed | tf_op | source)
XLA Modules:
  0.0 128.1 jit_solution(8473874139374876361)
XLA Ops:
  0.6 0.0 copy-start
  0.6 1.6 %copy-done = s32[4096,128]{1,0:T(8,128)S(1)} copy-done((s32[4096,128]{1,0:T(8,128)S(1)}, s32[4096,128]{1,0:T(8,128)}, u32[]{:S(2)}) %copy-start) | copy-done | bytes 2097176
  2.2 0.0 copy-start.1
  2.2 1.0 copy-done.1
  3.3 0.0 copy-start.2
  3.3 0.8 copy-done.2
  4.1 46.7 %shard_map.50 = (bf16[2048,4096]{1,0:T(8,128)(2,1)S(1)}, f32[2048,128]{1,0:T(8,128)S(1)}) custom-call(bf16[2048,128]{1,0:T(8,128)(2,1)S(1)} %copy-done.1, s32[3,4096]{1,0:T(4,128)S(1)} %copy-done.2, s32[4096,128]{1,0:T(8,128)S(1)} %copy-done), custom_call_target="tpu_custom_call" | custom-call | tf_op jit(solution)/shard_map/pallas_call | solution.py:155
  50.8 0.1 convert_element_type.8
  50.9 18.5 %shard_map.51 = bf16[4,512,128]{2,1,0:T(8,128)(2,1)S(1)} custom-call(bf16[4,512,128]{2,1,0:T(8,128)(2,1)S(1)} %bitcast.19), custom_call_target="tpu_custom_call" | custom-call | tf_op jit(solution)/shard_map/pallas_call | solution.py:235
  69.4 16.4 %shard_map.52 = (f32[128,128]{1,0:T(8,128)S(1)}, f32[128,4096]{1,0:T(8,128)S(1)}) custom-call(bf16[2048,128]{1,0:T(8,128)(2,1)S(1)} %bitcast.16, bf16[2048,4096]{1,0:T(8,128)(2,1)S(1)} %get-tuple-element.7.tile_ref), custom_call_target="tpu_custom_call" | custom-call | tf_op jit(solution)/shard_map/pallas_call | solution.py:290
  85.8 0.1 copy.5
  85.9 0.1 copy.6
  86.0 11.7 %cholesky.17 = f32[128,128]{1,0:T(8,128)S(1)} custom-call(f32[128,128]{1,0:T(8,128)S(1)} %fusion.3), custom_call_target="Cholesky" | custom-call | tf_op jit(solution)/shard_map/jit(cholesky)/cholesky | solution.py:365
  97.8 0.6 compare_reduce_fusion
  98.4 0.7 fusion.1
  99.1 9.8 %custom-call.6 = f32[1,128,128]{1,2,0:T(8,128)S(1)} custom-call(f32[1,128,128]{2,1,0:T(8,128)S(1)} %fusion.1), custom_call_target="InvertDiagBlocksLowerTriangular" | custom-call | tf_op jit(solution)/shard_map/triangular_solve | solution.py:366
  108.9 0.3 convolution_multiply_fusion.1
  109.1 1.9 %fusion = bf16[128,4096]{1,0:T(8,128)(2,1)S(1)} fusion(f32[128,128]{1,0:T(8,128)S(1)} %convolution_multiply_fusion.1, f32[128,4096]{1,0:T(8,128)S(1)} %get-tuple-element.9), kind=kOutput, calls=%fused_computation.1 | convolution fusion | flops 806354944 | bytes 3211264 | tf_op jit(solution)/shard_map/dot_general | solution.py:370
  111.1 14.8 %shard_map.53 = f32[16,4096]{1,0:T(8,128)S(1)} custom-call(bf16[8,16,4096]{2,1,0:T(8,128)(2,1)S(1)} %bitcast.18), custom_call_target="tpu_custom_call" | custom-call | tf_op jit(solution)/shard_map/pallas_call | solution.py:338
  125.9 1.6 %fusion.4 = f32[2048,128]{1,0:T(8,128)} fusion(bf16[2048,128]{1,0:T(8,128)(2,1)S(1)} %bitcast.17, f32[128,128]{1,0:T(8,128)S(1)} %convolution_multiply_fusion.1), kind=kOutput, calls=%fused_computation.13 | convolution fusion | flops 402653184 | bytes 1638400 | tf_op jit(solution)/shard_map/dot_general | solution.py:373
  127.4 0.7 copy.8
  (3 shorter events, 0.1 us)
Async XLA Ops:
  0.6 1.6 %copy-start = (s32[4096,128]{1,0:T(8,128)S(1)}, s32[4096,128]{1,0:T(8,128)}, u32[]{:S(2)}) copy-start(s32[4096,128]{1,0:T(8,128)} %sketch_ref.1) | copy-start | bytes 6291460
  2.2 1.0 copy-start.1
  3.3 0.8 copy-start.2

commit v2 on v1

--- a/solution.py
+++ b/solution.py
@@ -20,7 +20,8 @@
 
 
 def gather_kernel(
-    count, width, coeffs_ref, triples_ref, sketch_ref, tile_ref, sum_ref, blocks, sel_ref, signs_ref, own_sem, send_sem, recv_sem
+    count, width, coeffs_ref, triples_ref, sketch_ref, tile_ref, value_ref, blocks, sel_ref, signs_ref,
+    sum_ref, part_ref, slots, full_ref, own_sem, send_sem, recv_sem, to_sem, from_sem, out_sem, in_sem
 ):
     me = lax.axis_index("feat")
     rows, part = coeffs_ref.shape
@@ -43,27 +44,11 @@
 
         lax.fori_loop(0, tiles, one, 0)
 
-    barrier = pltpu.get_barrier_semaphore()
-
-    @pl.when(me > 0)
-    def _():
-        pl.semaphore_signal(barrier, inc=1, device_id={"feat": me - 1}, device_id_type=MESH)
-
-    @pl.when(me < count - 1)
-    def _():
-        pl.semaphore_signal(barrier, inc=1, device_id={"feat": me + 1}, device_id_type=MESH)
-
     own = pltpu.make_async_copy(coeffs_ref, blocks.at[me], own_sem)
     own.start()
-
-    @pl.when((me > 0) & (me < count - 1))
-    def _():
-        pl.semaphore_wait(barrier, 2)
-
-    @pl.when((me == 0) | (me == count - 1))
-    def _():
-        pl.semaphore_wait(barrier, 1)
-
+    peers = peers_of(me, count)
+    piece = step // count
+    greet("feat", peers)
     own.wait()
 
     def copy(side, hop, chunk, source, target):
@@ -77,6 +62,30 @@
             device_id_type=MESH,
         )
 
+    def rows_of(chunk, owner):
+        return pl.ds(pl.multiple_of(chunk * step + owner * piece, piece), piece)
+
+    def reduce_copy(k, chunk):
+        return pltpu.make_async_remote_copy(
+            src_ref=part_ref.at[rows_of(chunk, peers[k])],
+            dst_ref=slots.at[k, chunk],
+            send_sem=to_sem.at[k, chunk],
+            recv_sem=from_sem.at[k, chunk],
+            device_id={"feat": peers[k]},
+            device_id_type=MESH,
+        )
+
+    def spread_copy(k, chunk, owner):
+        span = full_ref.at[rows_of(chunk, owner)]
+        return pltpu.make_async_remote_copy(
+            src_ref=span,
+            dst_ref=span,
+            send_sem=out_sem.at[k, chunk],
+            recv_sem=in_sem.at[k, chunk],
+            device_id={"feat": peers[k]},
+            device_id_type=MESH,
+        )
+
     def one_round(turn, carry):
         for hop in range(count):
             chunk = turn - hop
@@ -107,11 +116,23 @@
             def _():
                 build(index)
 
-        @pl.when(turn >= count - 1)
+        base = turn - (count - 1)
+
+        @pl.when((base >= 1) & (base <= CHUNKS))
         def _():
-            first_row = pl.multiple_of((turn - (count - 1)) * step, step)
+            for k in range(count - 1):
+                reduce_copy(k, base - 1).start()
+
+        @pl.when(base >= 2)
+        def _():
+            for k in range(count - 1):
+                spread_copy(k, base - 2, me).start()
+
+        @pl.when((base >= 0) & (base < CHUNKS))
+        def _():
+            first_row = pl.multiple_of(base * step, step)
             here = pl.ds(first_row, step)
-            sum_ref[here, :] = jnp.zeros((step, sum_ref.shape[1]), jnp.float32)
+            sum_ref[...] = jnp.zeros(sum_ref.shape, jnp.float32)
             low = jnp.concatenate([blocks[s, here, :] for s in range(count // 2)], axis=1)
             high = jnp.concatenate([blocks[s, here, :] for s in range(count // 2, count)], axis=1)
             full = jnp.concatenate([low, high], axis=1)
@@ -123,16 +144,30 @@
                 third = jnp.dot(full, sel_ref[2 * half :, cols], preferred_element_type=jnp.float32)
                 tile = (first * second * third).astype(jnp.bfloat16)
                 tile_ref[here, cols] = tile
-                sum_ref[here, :] += jnp.dot(tile, signs_ref[cols, :], preferred_element_type=jnp.float32)
+                sum_ref[...] += jnp.dot(tile, signs_ref[cols, :], preferred_element_type=jnp.float32)
                 return unused
 
             lax.fori_loop(0, tiles, one_tile, 0, unroll=2)
+            part_ref[here, :] = sum_ref[...].astype(jnp.bfloat16)
+
+        @pl.when((base >= 1) & (base <= CHUNKS))
+        def _():
+            mine = rows_of(base - 1, me)
+            total = part_ref[mine, :].astype(jnp.float32)
+            for k in range(count - 1):
+                reduce_copy(k, base - 1).wait_recv()
+                total = total + slots[k, base - 1].astype(jnp.float32)
+            full_ref[mine, :] = total.astype(jnp.bfloat16)
 
         return carry
 
-    lax.fori_loop(0, CHUNKS + count - 1, one_round, 0)
+    lax.fori_loop(0, CHUNKS + count + 1, one_round, 0)
 
     def drain(chunk, carry):
+        for k in range(count - 1):
+            spread_copy(k, chunk, lax.rem(me + count - 1 - k, count)).wait_recv()
+            spread_copy(k, chunk, me).wait_send()
+            reduce_copy(k, chunk).wait_send()
         for hop in range(count - 1):
 
             @pl.when((me >= hop) & (me < count - 1))
@@ -146,28 +181,35 @@
         return carry
 
     lax.fori_loop(0, CHUNKS, drain, 0)
+    value_ref[...] = full_ref[...]
 
 
 def gather_features(coeffs, triples, sketch, count):
     rows, part = coeffs.shape
     feats, rank = sketch.shape
     hops = max(count - 1, 1)
+    step = rows // CHUNKS
     return pl.pallas_call(
         functools.partial(gather_kernel, count, min(512, feats)),
         in_specs=[VMEM] * 3,
         out_specs=[VMEM] * 2,
         out_shape=[
             jax.ShapeDtypeStruct((rows, feats), jnp.bfloat16),
-            jax.ShapeDtypeStruct((rows, rank), jnp.float32),
+            jax.ShapeDtypeStruct((rows, rank), jnp.bfloat16),
         ],
         scratch_shapes=[
             pltpu.VMEM((count, rows, part), jnp.bfloat16),
             pltpu.VMEM((2 * count * part, feats), jnp.bfloat16),
             pltpu.VMEM((feats, rank), jnp.bfloat16),
+            pltpu.VMEM((step, rank), jnp.float32),
+            pltpu.VMEM((rows, rank), jnp.bfloat16),
+            pltpu.VMEM((hops, CHUNKS, step // count, rank), jnp.bfloat16),
+            pltpu.VMEM((rows, rank), jnp.bfloat16),
             pltpu.SemaphoreType.DMA,
             pltpu.SemaphoreType.DMA((2, hops, CHUNKS)),
             pltpu.SemaphoreType.DMA((2, hops, CHUNKS)),
-        ],
+        ]
+        + [pltpu.SemaphoreType.DMA((hops, CHUNKS))] * 4,
         compiler_params=pltpu.CompilerParams(
             collective_id=0, has_side_effects=True, vmem_limit_bytes=24 << 20
         ),
@@ -176,75 +218,6 @@
 
 def peers_of(me, count):
     return [lax.rem(me + k, count) for k in range(1, count)]
-
-
-def sum_gather_kernel(count, part_ref, out_ref, slots, full, send_sem, recv_sem, send_again, recv_again):
-    me = lax.axis_index("feat")
-    peers = peers_of(me, count)
-    greet("feat", peers)
-    copies = []
-    for k, peer in enumerate(peers):
-        copies.append(
-            pltpu.make_async_remote_copy(
-                src_ref=part_ref.at[peer],
-                dst_ref=slots.at[k],
-                send_sem=send_sem.at[k],
-                recv_sem=recv_sem.at[k],
-                device_id={"feat": peer},
-                device_id_type=MESH,
-            )
-        )
-        copies[-1].start()
-    total = part_ref[me].astype(jnp.float32)
-    for k, copy in enumerate(copies):
-        copy.wait_recv()
-        total = total + slots[k].astype(jnp.float32)
-    full[me] = total.astype(full.dtype)
-    again = []
-    for k, peer in enumerate(peers):
-        again.append(
-            pltpu.make_async_remote_copy(
-                src_ref=full.at[me],
-                dst_ref=full.at[me],
-                send_sem=send_again.at[k],
-                recv_sem=recv_again.at[k],
-                device_id={"feat": peer},
-                device_id_type=MESH,
-            )
-        )
-        again[-1].start()
-    for k in range(count - 1):
-        source = lax.rem(me + count - 1 - k, count)
-        pltpu.make_async_remote_copy(
-            src_ref=full.at[source],
-            dst_ref=full.at[source],
-            send_sem=send_again.at[k],
-            recv_sem=recv_again.at[k],
-            device_id={"feat": peers[k]},
-            device_id_type=MESH,
-        ).wait_recv()
-    out_ref[...] = full[...]
-    for copy in copies + again:
-        copy.wait_send()
-
-
-def sum_gather(part, count):
-    rows, rank = part.shape
-    blocks = part.reshape(count, rows // count, rank)
-    others = max(count - 1, 1)
-    out = pl.pallas_call(
-        functools.partial(sum_gather_kernel, count),
-        in_specs=[VMEM],
-        out_specs=VMEM,
-        out_shape=jax.ShapeDtypeStruct(blocks.shape, part.dtype),
-        scratch_shapes=[
-            pltpu.VMEM((others,) + blocks.shape[1:], part.dtype),
-            pltpu.VMEM(blocks.shape, part.dtype),
-        ]
-        + [pltpu.SemaphoreType.DMA((others,))] * 4,
-        compiler_params=pltpu.CompilerParams(collective_id=1, has_side_effects=True, vmem_limit_bytes=8 << 20),
-    )(blocks)
-    return out.reshape(rows, rank)
 
 
 def gram_kernel(count, width, value_ref, tile_ref, gram_ref, raw_ref, turned, slots, send_sem, recv_sem):
@@ -357,8 +330,7 @@
     feat_count = lax.axis_size("feat")
     total_rows = rows_here * img_count
     total_feats = feats_here * feat_count
-    tiles, part = gather_features(coeffs, triples, sketch, feat_count)
-    value = sum_gather(part.astype(jnp.bfloat16), feat_count)
+    tiles, value = gather_features(coeffs, triples, sketch, feat_count)
     sketch_scale = (1.5 / total_feats) ** 0.5
     gram, raw = gram_and_raw(value, tiles, img_count)
     gram = gram * (sketch_scale * sketch_scale / total_rows)

time: 128 us -> 127 us (level)
  Pallas kernels: 96.4 us -> 94.7 us
    pallas_call x1 -> x0, Pallas kernels: 18.5 us -> none  [sum_gather(): pl.pallas_call(functools.partial(sum_gather_kernel, count), in_specs=[VME...]
    pallas_call x1, Pallas kernels: 46.7 us -> 59.8 us  [gather_features(): pl.pallas_call(functools.partial(gather_kernel, count, min(512, feats)),...]
    pallas_call x1, Pallas kernels: 16.4 us -> 20 us  [gram_and_raw(): pl.pallas_call(functools.partial(gram_kernel, count, min(512, feats)), in...]
where the time goes in v2:
time: 127 us; the launch traced here: 126 us
  Pallas kernels  94.7 us (75%)
  other arithmetic  22.9 us (18%)
  local copies, waits for them, and re-layouts  4.34 us (3%)
  matrix products  3.73 us (3%)
    pallas_call x1, Pallas kernels, gather_features(): pl.pallas_call(functools.partial(gather_kernel, count, min(512, feats)),...  59.8 us
    pallas_call x1, Pallas kernels, gram_and_raw(): pl.pallas_call(functools.partial(gram_kernel, count, min(512, feats)), in...  20 us
    pallas_call x1, Pallas kernels, sum_rows(): pl.pallas_call(functools.partial(rows_kernel, count), in_specs=[VMEM], ou...  14.8 us
    another operation x3, other arithmetic, on_device(): lower = jnp.linalg.cholesky(gram)  12.4 us
    another operation x2, other arithmetic, on_device(): lax.linalg.triangular_solve(lower, jnp.eye(rank_cols, dtype=jnp.float32),...  10.5 us
    unnamed x7, local copies, waits for them, and re-layouts  4.17 us

profile of v2, /device:TPU:1, one launch (start us, length us, event | category | flops | bytes accessed | tf_op | source)
XLA Modules:
  0.0 126.3 jit_solution(3643723183601751620)
XLA Ops:
  0.6 0.0 copy-start
  0.6 1.6 %copy-done = s32[4096,128]{1,0:T(8,128)S(1)} copy-done((s32[4096,128]{1,0:T(8,128)S(1)}, s32[4096,128]{1,0:T(8,128)}, u32[]{:S(2)}) %copy-start) | copy-done | bytes 2097176
  2.2 0.0 copy-start.1
  2.2 1.0 copy-done.1
  3.3 0.0 copy-start.2
  3.3 0.8 copy-done.2
  4.1 59.8 %shard_map.50 = (bf16[2048,4096]{1,0:T(8,128)(2,1)S(1)}, bf16[2048,128]{1,0:T(8,128)(2,1)S(1)}) custom-call(bf16[2048,128]{1,0:T(8,128)(2,1)S(1)} %copy-done.1, s32[3,4096]{1,0:T(4,128)S(1)} %copy-done.2, s32[4096,128]{1,0:T(8,128)S(1)} %copy-done), custom_call_target="tpu_custom_call" | custom-call | tf_op jit(solution)/shard_map/pallas_call | solution.py:192
  63.9 20.0 %shard_map.51 = (f32[128,128]{1,0:T(8,128)S(1)}, f32[128,4096]{1,0:T(8,128)S(1)}) custom-call(bf16[2048,128]{1,0:T(8,128)(2,1)S(1)} %get-tuple-element.6.value_ref, bf16[2048,4096]{1,0:T(8,128)(2,1)S(1)} %get-tuple-element.7.tile_ref), custom_call_target="tpu_custom_call" | custom-call | tf_op jit(solution)/shard_map/pallas_call | solution.py:263
  84.0 0.1 copy.5
  84.1 0.1 copy.6
  84.2 11.7 %cholesky.17 = f32[128,128]{1,0:T(8,128)S(1)} custom-call(f32[128,128]{1,0:T(8,128)S(1)} %fusion.3), custom_call_target="Cholesky" | custom-call | tf_op jit(solution)/shard_map/jit(cholesky)/cholesky | solution.py:337
  96.0 0.6 compare_reduce_fusion
  96.6 0.7 fusion.1
  97.3 9.8 %custom-call.6 = f32[1,128,128]{1,2,0:T(8,128)S(1)} custom-call(f32[1,128,128]{2,1,0:T(8,128)S(1)} %fusion.1), custom_call_target="InvertDiagBlocksLowerTriangular" | custom-call | tf_op jit(solution)/shard_map/triangular_solve | solution.py:338
  107.1 0.3 convolution_multiply_fusion.1
  107.3 1.9 %fusion = bf16[128,4096]{1,0:T(8,128)(2,1)S(1)} fusion(f32[128,128]{1,0:T(8,128)S(1)} %convolution_multiply_fusion.1, f32[128,4096]{1,0:T(8,128)S(1)} %get-tuple-element.9), kind=kOutput, calls=%fused_computation.1 | convolution fusion | flops 806354944 | bytes 3211264 | tf_op jit(solution)/shard_map/dot_general | solution.py:342
  109.3 14.8 %shard_map.52 = f32[16,4096]{1,0:T(8,128)S(1)} custom-call(bf16[8,16,4096]{2,1,0:T(8,128)(2,1)S(1)} %bitcast.14), custom_call_target="tpu_custom_call" | custom-call | tf_op jit(solution)/shard_map/pallas_call | solution.py:311
  124.1 1.6 %fusion.4 = f32[2048,128]{1,0:T(8,128)} fusion(bf16[2048,128]{1,0:T(8,128)(2,1)S(1)} %get-tuple-element.6.value_ref, f32[128,128]{1,0:T(8,128)S(1)} %convolution_multiply_fusion.1), kind=kOutput, calls=%fused_computation.13 | convolution fusion | flops 402653184 | bytes 1638400 | tf_op jit(solution)/shard_map/dot_general | solution.py:345
  125.6 0.7 copy.8
  (3 shorter events, 0.1 us)
Async XLA Ops:
  0.6 1.6 %copy-start = (s32[4096,128]{1,0:T(8,128)S(1)}, s32[4096,128]{1,0:T(8,128)}, u32[]{:S(2)}) copy-start(s32[4096,128]{1,0:T(8,128)} %sketch_ref.1) | copy-start | bytes 6291460
  2.2 1.0 copy-start.1
  3.3 0.8 copy-start.2

commit v3 on v2

--- a/solution.py
+++ b/solution.py
@@ -280,6 +280,39 @@
     )(value, tiles)
 
 
+def factor_kernel(scale, after, gram_ref, out_ref, left, right):
+    size = gram_ref.shape[0]
+    rows = lax.broadcasted_iota(jnp.int32, (size, size), 0)
+    lanes = lax.broadcasted_iota(jnp.int32, (size, size), 1)
+    left[...] = gram_ref[...] * scale
+    right[...] = jnp.where(rows == lanes, 1.0, 0.0)
+
+    def eliminate(j, carry):
+        block = left[...]
+        column = jnp.sum(jnp.where(lanes == j, block, 0.0), axis=1, keepdims=True)
+        pivot_row = left[pl.ds(j, 1), :]
+        pivot = jnp.sum(jnp.where(lanes[:1] == j, pivot_row, 0.0), axis=1, keepdims=True)
+        factor = jnp.where(rows[:, :1] > j, column / pivot, 0.0)
+        left[...] = block - factor * pivot_row
+        right[...] = right[...] - factor * right[pl.ds(j, 1), :]
+        return carry
+
+    lax.fori_loop(0, size, eliminate, 0)
+    diagonal = jnp.sum(jnp.where(rows == lanes, left[...], 0.0), axis=1, keepdims=True)
+    out_ref[...] = right[...] * (after / jnp.sqrt(diagonal))
+
+
+def inverse_factor(gram, scale, after):
+    return pl.pallas_call(
+        functools.partial(factor_kernel, scale, after),
+        in_specs=[VMEM],
+        out_specs=VMEM,
+        out_shape=jax.ShapeDtypeStruct(gram.shape, jnp.float32),
+        scratch_shapes=[pltpu.VMEM(gram.shape, jnp.float32)] * 2,
+        compiler_params=pltpu.CompilerParams(vmem_limit_bytes=8 << 20),
+    )(gram)
+
+
 def rows_kernel(count, part_ref, out_ref, slots, send_sem, recv_sem):
     me = lax.axis_index("img")
     peers = peers_of(me, count)
@@ -333,11 +366,7 @@
     tiles, value = gather_features(coeffs, triples, sketch, feat_count)
     sketch_scale = (1.5 / total_feats) ** 0.5
     gram, raw = gram_and_raw(value, tiles, img_count)
-    gram = gram * (sketch_scale * sketch_scale / total_rows)
-    lower = jnp.linalg.cholesky(gram)
-    inverse = lax.linalg.triangular_solve(
-        lower, jnp.eye(rank_cols, dtype=jnp.float32), left_side=True, lower=True
-    ) * sketch_scale
+    inverse = inverse_factor(gram, sketch_scale * sketch_scale / total_rows, sketch_scale)
     exact = lax.Precision.HIGHEST
     solved = jnp.dot(inverse, raw, precision=exact) / jnp.sqrt(jnp.float32(total_rows))
     outgoing = solved.astype(jnp.bfloat16).reshape(img_count, rank_cols // img_count, feats_here)

time: 127 us -> 117 us (0.921)
  other arithmetic: 22.9 us -> 0 us
  Pallas kernels: 94.7 us -> 108 us
    another operation x5 -> x0, other arithmetic: 22.9 us -> none  [the longest x3 12.4 us: on_device(): lower = jnp.linalg.cholesky(gram)]
    pallas_call x0 -> x1, Pallas kernels: none -> 13.4 us  [inverse_factor(): pl.pallas_call(functools.partial(factor_kernel, scale, after), in_specs=[...]
where the time goes in v3:
time: 117 us; the launch traced here: 116 us
  Pallas kernels  108 us (92%)
  local copies, waits for them, and re-layouts  4.17 us (4%)
  matrix products  3.48 us (3%)
    pallas_call x1, Pallas kernels, gather_features(): pl.pallas_call(functools.partial(gather_kernel, count, min(512, feats)),...  59.8 us
    pallas_call x1, Pallas kernels, gram_and_raw(): pl.pallas_call(functools.partial(gram_kernel, count, min(512, feats)), in...  20 us
    pallas_call x1, Pallas kernels, sum_rows(): pl.pallas_call(functools.partial(rows_kernel, count), in_specs=[VMEM], ou...  14.8 us
    pallas_call x1, Pallas kernels, inverse_factor(): pl.pallas_call(functools.partial(factor_kernel, scale, after), in_specs=[...  13.4 us
    unnamed x7, local copies, waits for them, and re-layouts  4.17 us

profile of v3, /device:TPU:1, one launch (start us, length us, event | category | flops | bytes accessed | tf_op | source)
XLA Modules:
  0.0 116.4 jit_solution(9839418782644381346)
XLA Ops:
  0.6 0.0 copy-start
  0.6 1.6 %copy-done = s32[4096,128]{1,0:T(8,128)S(1)} copy-done((s32[4096,128]{1,0:T(8,128)S(1)}, s32[4096,128]{1,0:T(8,128)}, u32[]{:S(2)}) %copy-start) | copy-done | bytes 2097176
  2.2 0.0 copy-start.1
  2.2 1.0 copy-done.1
  3.3 0.0 copy-start.2
  3.3 0.8 copy-done.2
  4.1 59.8 %shard_map.50 = (bf16[2048,4096]{1,0:T(8,128)(2,1)S(1)}, bf16[2048,128]{1,0:T(8,128)(2,1)S(1)}) custom-call(bf16[2048,128]{1,0:T(8,128)(2,1)S(1)} %copy-done.1, s32[3,4096]{1,0:T(4,128)S(1)} %copy-done.2, s32[4096,128]{1,0:T(8,128)S(1)} %copy-done), custom_call_target="tpu_custom_call" | custom-call | tf_op jit(solution)/shard_map/pallas_call | solution.py:192
  63.9 20.0 %shard_map.51 = (f32[128,128]{1,0:T(8,128)S(1)}, f32[128,4096]{1,0:T(8,128)S(1)}) custom-call(bf16[2048,128]{1,0:T(8,128)(2,1)S(1)} %get-tuple-element.6.value_ref, bf16[2048,4096]{1,0:T(8,128)(2,1)S(1)} %get-tuple-element.7.tile_ref), custom_call_target="tpu_custom_call" | custom-call | tf_op jit(solution)/shard_map/pallas_call | solution.py:263
  84.0 13.4 %shard_map.52 = f32[128,128]{1,0:T(8,128)S(1)} custom-call(f32[128,128]{1,0:T(8,128)S(1)} %get-tuple-element.8.gram_ref), custom_call_target="tpu_custom_call" | custom-call | tf_op jit(solution)/shard_map/pallas_call | solution.py:306
  97.4 1.9 %fusion = bf16[128,4096]{1,0:T(8,128)(2,1)S(1)} fusion(f32[128,128]{1,0:T(8,128)S(1)} %shard_map.52, f32[128,4096]{1,0:T(8,128)S(1)} %get-tuple-element.9), kind=kOutput, calls=%fused_computation.1 | convolution fusion | flops 806354944 | bytes 3211264 | tf_op jit(solution)/shard_map/dot_general | solution.py:371
  99.3 14.8 %shard_map.53 = f32[16,4096]{1,0:T(8,128)S(1)} custom-call(bf16[8,16,4096]{2,1,0:T(8,128)(2,1)S(1)} %bitcast.5), custom_call_target="tpu_custom_call" | custom-call | tf_op jit(solution)/shard_map/pallas_call | solution.py:344
  114.1 1.6 %fusion.1 = f32[2048,128]{1,0:T(8,128)} fusion(bf16[2048,128]{1,0:T(8,128)(2,1)S(1)} %get-tuple-element.6.value_ref, f32[128,128]{1,0:T(8,128)S(1)} %shard_map.52), kind=kOutput, calls=%fused_computation.2 | convolution fusion | flops 402653184 | bytes 1638400 | tf_op jit(solution)/shard_map/dot_general | solution.py:374
  115.7 0.7 copy.6
Async XLA Ops:
  0.6 1.6 %copy-start = (s32[4096,128]{1,0:T(8,128)S(1)}, s32[4096,128]{1,0:T(8,128)}, u32[]{:S(2)}) copy-start(s32[4096,128]{1,0:T(8,128)} %sketch_ref.1) | copy-start | bytes 6291460
  2.2 1.0 copy-start.1
  3.3 0.8 copy-start.2

commit v4 on v3

--- a/solution.py
+++ b/solution.py
@@ -297,7 +297,7 @@
         right[...] = right[...] - factor * right[pl.ds(j, 1), :]
         return carry
 
-    lax.fori_loop(0, size, eliminate, 0)
+    lax.fori_loop(0, size, eliminate, 0, unroll=4)
     diagonal = jnp.sum(jnp.where(rows == lanes, left[...], 0.0), axis=1, keepdims=True)
     out_ref[...] = right[...] * (after / jnp.sqrt(diagonal))
 

time: 117 us -> 117 us (level)
  no operation moved by 1% of the time
where the time goes in v4:
time: 117 us
  Pallas kernels  108 us (92%)
  local copies, waits for them, and re-layouts  4.17 us (4%)
  matrix products  3.48 us (3%)
    pallas_call x1, Pallas kernels, gather_features(): pl.pallas_call(functools.partial(gather_kernel, count, min(512, feats)),...  59.8 us
    pallas_call x1, Pallas kernels, gram_and_raw(): pl.pallas_call(functools.partial(gram_kernel, count, min(512, feats)), in...  20 us
    pallas_call x1, Pallas kernels, sum_rows(): pl.pallas_call(functools.partial(rows_kernel, count), in_specs=[VMEM], ou...  14.8 us
    pallas_call x1, Pallas kernels, inverse_factor(): pl.pallas_call(functools.partial(factor_kernel, scale, after), in_specs=[...  13.5 us
    unnamed x7, local copies, waits for them, and re-layouts  4.17 us

profile of v4, /device:TPU:1, one launch (start us, length us, event | category | flops | bytes accessed | tf_op | source)
XLA Modules:
  0.0 116.5 jit_solution(15652000777522123638)
XLA Ops:
  0.6 0.0 copy-start
  0.6 1.6 %copy-done = s32[4096,128]{1,0:T(8,128)S(1)} copy-done((s32[4096,128]{1,0:T(8,128)S(1)}, s32[4096,128]{1,0:T(8,128)}, u32[]{:S(2)}) %copy-start) | copy-done | bytes 2097176
  2.2 0.0 copy-start.1
  2.2 1.0 copy-done.1
  3.3 0.0 copy-start.2
  3.3 0.8 copy-done.2
  4.1 59.8 %shard_map.50 = (bf16[2048,4096]{1,0:T(8,128)(2,1)S(1)}, bf16[2048,128]{1,0:T(8,128)(2,1)S(1)}) custom-call(bf16[2048,128]{1,0:T(8,128)(2,1)S(1)} %copy-done.1, s32[3,4096]{1,0:T(4,128)S(1)} %copy-done.2, s32[4096,128]{1,0:T(8,128)S(1)} %copy-done), custom_call_target="tpu_custom_call" | custom-call | tf_op jit(solution)/shard_map/pallas_call | solution.py:192
  63.9 20.0 %shard_map.51 = (f32[128,128]{1,0:T(8,128)S(1)}, f32[128,4096]{1,0:T(8,128)S(1)}) custom-call(bf16[2048,128]{1,0:T(8,128)(2,1)S(1)} %get-tuple-element.6.value_ref, bf16[2048,4096]{1,0:T(8,128)(2,1)S(1)} %get-tuple-element.7.tile_ref), custom_call_target="tpu_custom_call" | custom-call | tf_op jit(solution)/shard_map/pallas_call | solution.py:263
  84.0 13.5 %shard_map.52 = f32[128,128]{1,0:T(8,128)S(1)} custom-call(f32[128,128]{1,0:T(8,128)S(1)} %get-tuple-element.8.gram_ref), custom_call_target="tpu_custom_call" | custom-call | tf_op jit(solution)/shard_map/pallas_call | solution.py:306
  97.5 1.9 %fusion = bf16[128,4096]{1,0:T(8,128)(2,1)S(1)} fusion(f32[128,128]{1,0:T(8,128)S(1)} %shard_map.52, f32[128,4096]{1,0:T(8,128)S(1)} %get-tuple-element.9), kind=kOutput, calls=%fused_computation.1 | convolution fusion | flops 806354944 | bytes 3211264 | tf_op jit(solution)/shard_map/dot_general | solution.py:371
  99.5 14.8 %shard_map.53 = f32[16,4096]{1,0:T(8,128)S(1)} custom-call(bf16[8,16,4096]{2,1,0:T(8,128)(2,1)S(1)} %bitcast.5), custom_call_target="tpu_custom_call" | custom-call | tf_op jit(solution)/shard_map/pallas_call | solution.py:344
  114.3 1.6 %fusion.1 = f32[2048,128]{1,0:T(8,128)} fusion(bf16[2048,128]{1,0:T(8,128)(2,1)S(1)} %get-tuple-element.6.value_ref, f32[128,128]{1,0:T(8,128)S(1)} %shard_map.52), kind=kOutput, calls=%fused_computation.2 | convolution fusion | flops 402653184 | bytes 1638400 | tf_op jit(solution)/shard_map/dot_general | solution.py:374
  115.8 0.7 copy.6
Async XLA Ops:
  0.6 1.6 %copy-start = (s32[4096,128]{1,0:T(8,128)S(1)}, s32[4096,128]{1,0:T(8,128)}, u32[]{:S(2)}) copy-start(s32[4096,128]{1,0:T(8,128)} %sketch_ref.1) | copy-start | bytes 6291460
  2.2 1.0 copy-start.1
  3.3 0.8 copy-start.2
